TPU v7x, 32 devices: a whole 2x2x4 slice. The times are simulated.
32 devices in a mesh: strike: 8 (over y, x, core), dip: 4 (over z).
Axes of the slice: x: 2, y: 2, z: 4, core: 2. Of those that a mesh axis runs over, the one named last changes fastest.
Arguments:
- slip: float32 [8192, 2048], P('strike', 'dip'), may hold values from -4 to 8
- slip_rate: float32 [8192, 2048], P('strike', 'dip'), may hold values from -6 to 6
- state: float32 [8192, 2048], P('strike', 'dip'), may hold values from -1 to 1
- loading: float32 [8192, 2048], P('strike', 'dip'), may hold values from -8 to 8
- normal_stress: float32 [8192, 2048], P('strike', 'dip'), may hold values from 0.5 to 2
- patch: int32 [8192, 2048], P('strike', 'dip'), may hold values from 0 to 3
- rate_coef: float32 [4], replicated, may hold values from 0.3 to 1
- state_coef: float32 [4], replicated, may hold values from 0.3 to 1
- slip_scale: float32 [4], replicated, may hold values from 0.5 to 2
- kernel: bfloat16 [16, 2048, 8192], P(None, ('strike', 'dip')), may hold values from -1.5 to 1.5
- history: bfloat16 [16, 2, 2048, 8192], P(None, None, ('strike', 'dip')), may hold values from -6 to 6
Outputs:
- new_rate: float32 [8192, 2048], P('strike', 'dip')
- new_state: float32 [8192, 2048], P('strike', 'dip')
- transfer_stress: float32 [8192, 2048], P('strike', 'dip')
- rate_modes: bfloat16 [2, 2048, 8192], P(None, ('strike', 'dip'))
All inputs are finite; a program needn't handle non-finite values.
Results may differ from a plain program's by a relative error of at most 0.001.
Values sent between devices are 32-bit elements; how exact they have to be, the bound alone decides.
A program may use at most 192 MiB of HBM per device.

v0:
```python
import math

import jax
import jax.numpy as jnp
from jax import lax
from jax.sharding import PartitionSpec as P

NEWTON = 8


shear_modulus = 1.0
damping = 0.5
relaxation = 0.35
time_step = 0.1


def inverse_sinh(value):
    size_v = jnp.abs(value)
    square = size_v * size_v
    result = jnp.log1p(size_v + square / (1.0 + jnp.sqrt(square + 1.0)))
    return jnp.where(value < 0.0, -result, result)


def tables(count_in, count_out, modulus, sign):
    row_index = lax.broadcasted_iota(jnp.int32, (count_in, count_out), 0)
    col_index = lax.broadcasted_iota(jnp.int32, (count_in, count_out), 1)
    angles = 2.0 * math.pi / modulus * (row_index * col_index % modulus).astype(jnp.float32)
    return (jnp.cos(angles), sign * jnp.sin(angles))


def cproduct(pattern, part_re, part_im, table_re, table_im):

    def product(left_op, right_op):
        return jnp.einsum(pattern, left_op, right_op, precision=lax.Precision.HIGHEST)

    if part_im is None:
        return (product(part_re, table_re), product(part_re, table_im))
    return (
        product(part_re, table_re) - product(part_im, table_im),
        product(part_re, table_im) + product(part_im, table_re),
    )


def factors(length):
    inner_len = 128
    return (length // inner_len, inner_len)


def transform_rows(part_re, part_im, sign, flipped):
    row_count, length = part_re.shape
    outer_len, inner_len = factors(length)
    part_re = part_re.reshape(row_count, outer_len, inner_len)
    if part_im is not None:
        part_im = part_im.reshape(row_count, outer_len, inner_len)
    first_re, first_im = tables(outer_len, outer_len, outer_len, sign)
    part_re, part_im = cproduct("rab,ac->rcb", part_re, part_im, first_re, first_im)
    twist_re, twist_im = tables(outer_len, inner_len, length, sign)
    part_re, part_im = (
        part_re * twist_re - part_im * twist_im,
        part_re * twist_im + part_im * twist_re,
    )
    second_re, second_im = tables(inner_len, inner_len, inner_len, sign)
    pattern = "rcb,bm->mcr" if flipped else "rcb,bm->rmc"
    part_re, part_im = cproduct(pattern, part_re, part_im, second_re, second_im)
    out_shape = (length, row_count) if flipped else (row_count, length)
    factor = 1.0 / math.sqrt(length)
    return (part_re.reshape(out_shape) * factor, part_im.reshape(out_shape) * factor)


def transform_cols(part_re, part_im, sign):
    length, col_count = part_re.shape
    outer_len, inner_len = factors(length)
    part_re = part_re.reshape(outer_len, inner_len, col_count)
    part_im = part_im.reshape(outer_len, inner_len, col_count)
    first_re, first_im = tables(outer_len, outer_len, outer_len, sign)
    part_re, part_im = cproduct("abr,ac->cbr", part_re, part_im, first_re, first_im)
    twist_re, twist_im = tables(outer_len, inner_len, length, sign)
    twist_re = twist_re[:, :, None]
    twist_im = twist_im[:, :, None]
    part_re, part_im = (
        part_re * twist_re - part_im * twist_im,
        part_re * twist_im + part_im * twist_re,
    )
    second_re, second_im = tables(inner_len, inner_len, inner_len, sign)
    part_re, part_im = cproduct("cbr,bm->rmc", part_re, part_im, second_re, second_im)
    factor = 1.0 / math.sqrt(length)
    return (
        part_re.reshape(col_count, length) * factor,
        part_im.reshape(col_count, length) * factor,
    )


def wavenumber(index, count):
    return 2.0 * math.pi / count * ((index + count // 2) % count - count // 2).astype(jnp.float32)


def lookup(patch, table):
    result = jnp.zeros(patch.shape, jnp.float32)
    for label in range(table.shape[0]):
        result = jnp.where(patch == label, table[label], result)
    return result


def friction(slip_rate, state, loading, normal_stress, transfer, coef_a, coef_b, length_l):
    stress = loading + transfer
    prefix = 2.0 * jnp.exp(-state / coef_a)
    angle_w = inverse_sinh(slip_rate / prefix)
    for iteration in range(NEWTON):
        residue = normal_stress * coef_a * angle_w + damping * prefix * jnp.sinh(angle_w) - stress
        slope = normal_stress * coef_a + damping * prefix * jnp.cosh(angle_w)
        ratio = residue / slope
        angle_w = angle_w - relaxation * ratio / (1.0 + jnp.abs(ratio))
    new_rate = prefix * jnp.sinh(angle_w)
    new_state = state + time_step * (coef_b / length_l) * (
        jnp.exp(-state / coef_b) - jnp.abs(new_rate)
    )
    return (new_rate, new_state)


def per_device(
    slip,
    slip_rate,
    state,
    loading,
    normal_stress,
    patch,
    rate_coef,
    state_coef,
    slip_scale,
    kernel,
    history,
):
    strike_count = lax.axis_size("strike")
    dip_count = lax.axis_size("dip")
    slip_rows, rate_rows = (
        lax.all_to_all(slip, "dip", split_axis=0, concat_axis=1, tiled=True),
        lax.all_to_all(slip_rate, "dip", split_axis=0, concat_axis=1, tiled=True),
    )
    slip_re, slip_im = transform_rows(slip_rows, None, -1.0, True)
    rate_re, rate_im = transform_rows(rate_rows, None, -1.0, True)
    pieces = (
        lax.all_to_all(slip_re, ("strike", "dip"), split_axis=0, concat_axis=1, tiled=True),
        lax.all_to_all(slip_im, ("strike", "dip"), split_axis=0, concat_axis=1, tiled=True),
        lax.all_to_all(rate_re, ("strike", "dip"), split_axis=0, concat_axis=1, tiled=True),
        lax.all_to_all(rate_im, ("strike", "dip"), split_axis=0, concat_axis=1, tiled=True),
    )
    slip_re, slip_im = transform_rows(pieces[0], pieces[1], -1.0, False)
    rate_re, rate_im = transform_rows(pieces[2], pieces[3], -1.0, False)
    band, total_x = slip_re.shape
    total_y = band * strike_count * dip_count
    offset = (lax.axis_index("strike") * dip_count + lax.axis_index("dip")) * band
    wave_y = wavenumber(offset + lax.broadcasted_iota(jnp.int32, (band,), 0), total_y)
    wave_x = wavenumber(lax.broadcasted_iota(jnp.int32, (total_x,), 0), total_x)
    magnitude = jnp.sqrt(wave_y[:, None] ** 2 + wave_x[None, :] ** 2)
    memory_re = jnp.einsum("jrc,jrc->rc", kernel, history[:, 0], preferred_element_type=jnp.float32)
    memory_im = jnp.einsum("jrc,jrc->rc", kernel, history[:, 1], preferred_element_type=jnp.float32)
    static = -0.5 * shear_modulus * magnitude
    stress_re = static * slip_re + memory_re
    stress_im = static * slip_im + memory_im
    rate_modes = jnp.stack([rate_re, rate_im]).astype(jnp.bfloat16)
    back_re, back_im = transform_rows(stress_re, stress_im, 1.0, False)
    back = (
        lax.all_to_all(back_re, ("strike", "dip"), split_axis=1, concat_axis=0, tiled=True),
        lax.all_to_all(back_im, ("strike", "dip"), split_axis=1, concat_axis=0, tiled=True),
    )
    line_re, line_im = transform_cols(back[0], back[1], 1.0)
    transfer = lax.all_to_all(line_re, "dip", split_axis=1, concat_axis=0, tiled=True)
    coef_a = lookup(patch, rate_coef)
    coef_b = lookup(patch, state_coef)
    length_l = lookup(patch, slip_scale)
    new_rate, new_state = friction(
        slip_rate, state, loading, normal_stress, transfer, coef_a, coef_b, length_l
    )
    return (new_rate, new_state, transfer, rate_modes)


def solution(mesh):
    return jax.shard_map(
        per_device,
        mesh=mesh,
        in_specs=(
            P("strike", "dip"),
            P("strike", "dip"),
            P("strike", "dip"),
            P("strike", "dip"),
            P("strike", "dip"),
            P("strike", "dip"),
            P(),
            P(),
            P(),
            P(None, ("strike", "dip"), None),
            P(None, None, ("strike", "dip"), None),
        ),
        out_specs=(
            P("strike", "dip"),
            P("strike", "dip"),
            P("strike", "dip"),
            P(None, ("strike", "dip"), None),
        ),
        check_vma=False,
    )
```

profile of v0, /device:TPU:0, one launch (start us, length us, event | category | flops | bytes accessed | tf_op | source)
XLA Modules:
  0.0 581.7 jit_solution(3470144887140389631)
XLA Ops:
  0.6 54.6 %all_to_all.126 = f32[4,256,512]{2,1,0:T(8,128)S(1)} all-to-all(f32[4,256,512]{2,1,0:T(8,128)} %bitcast.262), channel_id=1, replica_groups=mesh['strike'=8,'dip'=4] {'dip'}, dimensions={0} | all-to-all | bytes 4194304 | tf_op jit(solution)/shard_map/all_to_all | solution.py:137
  55.2 4.5 all-to-all-start
  71.0 36.1 %all-to-all-done = f32[4,256,512]{2,1,0:T(8,128)} async-done(((f32[4,256,512]{2,1,0:T(8,128)}), f32[4,256,512]{2,1,0:T(8,128)}, u32[]{:S(2)}, u32[]{:S(2)}) %all-to-all-start) | async-done | bytes 2097184 | tf_op jit(solution)/shard_map/all_to_all | solution.py:136
  107.1 4.3 copy.130
  116.7 5.5 subtract_bitcast_fusion
  130.2 4.3 all-to-all-start.2
  134.5 4.4 fusion.99
  144.2 37.2 %all-to-all-done.2 = f32[32,64,256]{2,1,0:T(8,128)} async-done(((f32[32,64,256]{2,1,0:T(8,128)}), f32[32,64,256]{2,1,0:T(8,128)}, u32[]{:S(2)}, u32[]{:S(2)}) %all-to-all-start.2) | async-done | bytes 2097184 | tf_op jit(solution)/shard_map/all_to_all | solution.py:143
  181.4 4.7 all-to-all-start.1
  186.4 4.2 fusion.83
  195.9 36.8 %all-to-all-done.1 = f32[32,64,256]{2,1,0:T(8,128)} async-done(((f32[32,64,256]{2,1,0:T(8,128)}), f32[32,64,256]{2,1,0:T(8,128)}, u32[]{:S(2)}, u32[]{:S(2)}) %all-to-all-start.1) | async-done | bytes 2097184 | tf_op jit(solution)/shard_map/all_to_all | solution.py:142
  232.7 5.2 all-to-all-start.7
  238.0 20.0 %fusion.1 = (f32[64,8192]{1,0:T(8,128)}, f32[64,8192]{1,0:T(8,128)}) fusion(bf16[16,64,8192]{2,1,0:T(8,128)(2,1)} %param.20, bf16[16,2,64,8192]{3,2,1,0:T(8,128)(2,1)} %param.21), kind=kLoop, calls=%fused_computation.3 | loop fusion | flops 57671680 | bytes 54525952 | tf_op jit(solution)/shard_map/jrc,jrc->rc/dot_general | solution.py:156
  257.9 4.2 fusion.81
  287.5 6.5 %all-to-all-start.8 = ((f32[32,64,256]{2,1,0:T(8,128)}), f32[32,64,256]{2,1,0:T(8,128)}, u32[]{:S(2)}, u32[]{:S(2)}) async-start(f32[32,64,256]{2,1,0:T(8,128)} %bitcast.255), calls=%async_computation.8 | async-start | bytes 4194304 | tf_op jit(solution)/shard_map/all_to_all | solution.py:145
  305.3 4.8 mul.985
  321.4 5.1 mul.989
  349.8 4.8 mul.1001
  358.7 6.1 %all-to-all-start.4 = ((f32[64,32,256]{2,0,1:T(8,128)}), f32[64,32,256]{2,0,1:T(8,128)}, u32[]{:S(2)}, u32[]{:S(2)}) async-start(f32[64,32,256]{2,0,1:T(8,128)} %copy.149), calls=%async_computation.4 | async-start | bytes 4194304 | tf_op jit(solution)/shard_map/all_to_all | solution.py:164
  382.1 29.6 %all-to-all-done.4 = f32[64,32,256]{2,0,1:T(8,128)} async-done(((f32[64,32,256]{2,0,1:T(8,128)}), f32[64,32,256]{2,0,1:T(8,128)}, u32[]{:S(2)}, u32[]{:S(2)}) %all-to-all-start.4) | async-done | bytes 2097184 | tf_op jit(solution)/shard_map/all_to_all | solution.py:164
  411.7 4.7 all-to-all-start.3
  420.9 4.1 copy.167
  426.7 4.9 copy.173
  438.6 5.7 fusion.91
  444.3 5.7 fusion.89
  450.0 13.1 %all-to-all-done.3 = f32[64,32,256]{2,0,1:T(8,128)} async-done(((f32[64,32,256]{2,0,1:T(8,128)}), f32[64,32,256]{2,0,1:T(8,128)}, u32[]{:S(2)}, u32[]{:S(2)}) %all-to-all-start.3) | async-done | bytes 2097184 | tf_op jit(solution)/shard_map/all_to_all | solution.py:163
  463.1 5.5 fusion.109
  468.6 5.3 multiply_subtract_fusion.1
  483.1 5.5 all-to-all-start.5
  500.7 4.3 mul.1062
  517.5 20.6 %all-to-all-done.5 = f32[256,4,512]{0,2,1:T(8,128)} async-done(((f32[256,4,512]{0,2,1:T(8,128)}), f32[256,4,512]{0,2,1:T(8,128)}, u32[]{:S(2)}, u32[]{:S(2)}) %all-to-all-start.5) | async-done | bytes 2097184 | tf_op jit(solution)/shard_map/all_to_all | solution.py:167
  541.1 40.4 %multiply_add_fusion.1 = (f32[1024,512]{1,0:T(8,128)}, f32[1024,512]{1,0:T(8,128)}) fusion(f32[1024,512]{1,0:T(8,128)} %param.13, pred[1024,512]{1,0:T(8,128)(4,1)} %get-tuple-element.16, pred[1024,512]{1,0:T(8,128)(4,1)S(1)} %copy-done.22, pred[1024,512]{1,0:T(8,128)(4,1)} %get-tuple-element.17, pred[1024,512]{1,0:T(8,128)(4,1)S(1)} %copy-done.21, ...), kind=kLoop, calls=%fused_computation.102 | loop fusion | flops 120061952 | bytes 16777264 | tf_op jit(solution)/shard_map/add | solution.py:114
  (129 shorter events, 177.7 us)
Async XLA Ops:
  55.2 51.9 %all-to-all-start = ((f32[4,256,512]{2,1,0:T(8,128)}), f32[4,256,512]{2,1,0:T(8,128)}, u32[]{:S(2)}, u32[]{:S(2)}) async-start(f32[4,256,512]{2,1,0:T(8,128)} %bitcast.261), calls=%async_computation | async-start | bytes 4194304 | tf_op jit(solution)/shard_map/all_to_all | solution.py:136
  113.7 2.4 copy-start.15
  113.7 3.0 copy-start.16
  122.2 2.6 copy-start.11
  122.2 2.6 copy-start.6
  130.2 51.2 %all-to-all-start.2 = ((f32[32,64,256]{2,1,0:T(8,128)}), f32[32,64,256]{2,1,0:T(8,128)}, u32[]{:S(2)}, u32[]{:S(2)}) async-start(f32[32,64,256]{2,1,0:T(8,128)} %bitcast.259), calls=%async_computation.2 | async-start | bytes 4194304 | tf_op jit(solution)/shard_map/all_to_all | solution.py:143
  134.5 4.4 copy-start.7
  181.4 51.4 %all-to-all-start.1 = ((f32[32,64,256]{2,1,0:T(8,128)}), f32[32,64,256]{2,1,0:T(8,128)}, u32[]{:S(2)}, u32[]{:S(2)}) async-start(f32[32,64,256]{2,1,0:T(8,128)} %bitcast.256), calls=%async_computation.1 | async-start | bytes 4194304 | tf_op jit(solution)/shard_map/all_to_all | solution.py:142
  232.7 54.8 %all-to-all-start.7 = ((f32[32,64,256]{2,1,0:T(8,128)}), f32[32,64,256]{2,1,0:T(8,128)}, u32[]{:S(2)}, u32[]{:S(2)}) async-start(f32[32,64,256]{2,1,0:T(8,128)} %bitcast.257), calls=%async_computation.7 | async-start | bytes 4194304 | tf_op jit(solution)/shard_map/all_to_all | solution.py:144
  279.8 2.1 copy-start.10
  287.5 71.2 %all-to-all-start.8 = ((f32[32,64,256]{2,1,0:T(8,128)}), f32[32,64,256]{2,1,0:T(8,128)}, u32[]{:S(2)}, u32[]{:S(2)}) async-start(f32[32,64,256]{2,1,0:T(8,128)} %bitcast.255), calls=%async_computation.8 | async-start | bytes 4194304 | tf_op jit(solution)/shard_map/all_to_all | solution.py:145
  294.0 3.9 copy-start.4
  310.1 3.9 copy-start.5
  321.4 5.1 copy-start.14
  339.7 2.2 copy-start.2
  358.7 53.0 %all-to-all-start.4 = ((f32[64,32,256]{2,0,1:T(8,128)}), f32[64,32,256]{2,0,1:T(8,128)}, u32[]{:S(2)}, u32[]{:S(2)}) async-start(f32[64,32,256]{2,0,1:T(8,128)} %copy.149), calls=%async_computation.4 | async-start | bytes 4194304 | tf_op jit(solution)/shard_map/all_to_all | solution.py:164
  364.8 3.9 copy-start.3
  382.1 34.6 %copy-start.23 = (f32[4]{0:T(128)S(1)}, f32[4]{0:T(128)}, u32[]{:S(2)}) copy-start(f32[4]{0:T(128)} %param.17) | copy-start | bytes 52
  382.1 35.2 %copy-start.24 = (f32[4]{0:T(128)S(1)}, f32[4]{0:T(128)}, u32[]{:S(2)}) copy-start(f32[4]{0:T(128)} %param.18) | copy-start | bytes 52
  382.1 35.9 %copy-start.25 = (f32[4]{0:T(128)S(1)}, f32[4]{0:T(128)}, u32[]{:S(2)}) copy-start(f32[4]{0:T(128)} %param.19) | copy-start | bytes 52
  382.1 36.6 %copy-start.19 = (s32[1024,512]{1,0:T(8,128)S(1)}, s32[1024,512]{1,0:T(8,128)}, u32[]{:S(2)}) copy-start(s32[1024,512]{1,0:T(8,128)} %param.16) | copy-start | bytes 6291460
  411.7 51.4 %all-to-all-start.3 = ((f32[64,32,256]{2,0,1:T(8,128)}), f32[64,32,256]{2,0,1:T(8,128)}, u32[]{:S(2)}, u32[]{:S(2)}) async-start(f32[64,32,256]{2,0,1:T(8,128)} %copy.146), calls=%async_computation.3 | async-start | bytes 4194304 | tf_op jit(solution)/shard_map/all_to_all | solution.py:163
  426.7 7.7 %copy-start.13 = (f32[64,64,128]{2,1,0:T(8,128)}, f32[64,64,128]{2,1,0:T(8,128)S(1)}, u32[]{:S(2)}) copy-start(f32[64,64,128]{2,1,0:T(8,128)S(1)} %reshape.268) | copy-start | bytes 6291460
  463.1 5.5 copy-start.17
  483.1 54.9 %all-to-all-start.5 = ((f32[256,4,512]{0,2,1:T(8,128)}), f32[256,4,512]{0,2,1:T(8,128)}, u32[]{:S(2)}, u32[]{:S(2)}) async-start(f32[256,4,512]{0,2,1:T(8,128)} %bitcast.258), calls=%async_computation.5 | async-start | bytes 4194304 | tf_op jit(solution)/shard_map/all_to_all | solution.py:167
  488.6 3.8 copy-start.9
  494.5 2.2 copy-start
  505.0 3.9 copy-start.1
  512.2 2.5 copy-start.18
  538.1 3.0 copy-start.20
  538.1 3.0 copy-start.21
  538.1 3.0 copy-start.22
  (2 other events, 4.1 us)
where the time goes:
time: 590 us; the launch traced here: 582 us
  waiting for transfers between devices  173 us (29%)
  matrix products  137 us (23%)
  local copies, waits for them, and re-layouts  105 us (18%)
  other arithmetic  69.7 us (12%)
  blocking collectives  54.6 us (9%)
  starting transfers between devices  41.4 us (7%)
    dot_general x42, matrix products, product(): jnp.einsum(pattern, left_op, right_op, precision=lax.Precision.HIGHEST)  137 us
    all_to_all x1, blocking collectives, per_device(): lax.all_to_all(slip_rate, 'dip', split_axis=0, concat_axis=1, tiled=True)  54.6 us
    add x1, other arithmetic, friction(): state + time_step * (coef_b / length_l) * (jnp.exp(-state / coef_b) - jnp...  40.4 us
    all_to_all x1, waiting for transfers between devices, per_device(): lax.all_to_all(slip_im, ('strike', 'dip'), split_axis=0, concat_axis=1, t...  37.2 us
    all_to_all x1, waiting for transfers between devices, per_device(): lax.all_to_all(slip_re, ('strike', 'dip'), split_axis=0, concat_axis=1, t...  36.8 us
    all_to_all x1, waiting for transfers between devices, per_device(): lax.all_to_all(slip, 'dip', split_axis=0, concat_axis=1, tiled=True)  36.1 us
    mul x9, local copies, waits for them, and re-layouts, transform_rows(): part_im.reshape(out_shape) * factor  30.5 us
    mul x9, local copies, waits for them, and re-layouts, transform_rows(): part_re.reshape(out_shape) * factor  29.6 us
  transfers between devices with their start and end apart: 8, of which 6 were waited for; matrix products, arithmetic and copies ran while one was open for 39% of the time, Pallas kernels for 0%

commit v1 on v0

v1 whole, which is shorter than its diff:
```python
import math

import jax
import jax.numpy as jnp
from jax import lax
from jax.sharding import PartitionSpec as P

NEWTON = 8


shear_modulus = 1.0
damping = 0.5
relaxation = 0.35
time_step = 0.1


def inverse_sinh(value):
    size_v = jnp.abs(value)
    square = size_v * size_v
    result = jnp.log1p(size_v + square / (1.0 + jnp.sqrt(square + 1.0)))
    return jnp.where(value < 0.0, -result, result)


def exact_tables(rows, cols, modulus, sign):
    angles = 2.0 * math.pi / modulus * (rows * cols % modulus).astype(jnp.float32)
    return (jnp.cos(angles), sign * jnp.sin(angles))


def grid_tables(count_in, count_out, modulus, sign):
    row_index = lax.broadcasted_iota(jnp.int32, (count_in, count_out), 0)
    col_index = lax.broadcasted_iota(jnp.int32, (count_in, count_out), 1)
    return exact_tables(row_index, col_index, modulus, sign)


def complex_table(count, sign, scale=1.0):
    cos, sin = grid_tables(count, count, count, sign)
    cos, sin = cos * scale, sin * scale
    return jnp.stack([jnp.stack([cos, sin], 1), jnp.stack([-sin, cos], 1)], 0)


def product(pattern, left_op, right_op):
    return jnp.einsum(pattern, left_op, right_op, precision=lax.Precision.HIGH)


def twist(part_re, part_im, table_re, table_im):
    return (
        part_re * table_re - part_im * table_im,
        part_re * table_im + part_im * table_re,
    )


INNER = 128


def wavenumber(index, count):
    return 2.0 * math.pi / count * ((index + count // 2) % count - count // 2).astype(jnp.float32)


def lookup(patch, table):
    result = jnp.zeros(patch.shape, jnp.float32)
    for label in range(table.shape[0]):
        result = jnp.where(patch == label, table[label], result)
    return result


def friction(slip_rate, state, loading, normal_stress, transfer, coef_a, coef_b, length_l):
    stress = loading + transfer
    prefix = 2.0 * jnp.exp(-state / coef_a)
    angle_w = inverse_sinh(slip_rate / prefix)
    weight = normal_stress * coef_a
    half = 0.5 * damping * prefix
    for iteration in range(NEWTON):
        grow = half * jnp.exp(angle_w)
        decay = half * jnp.exp(-angle_w)
        residue = weight * angle_w + (grow - decay) - stress
        slope = weight + (grow + decay)
        angle_w = angle_w - relaxation * residue / (slope + jnp.abs(residue))
    new_rate = prefix * jnp.sinh(angle_w)
    new_state = state + time_step * (coef_b / length_l) * (
        jnp.exp(-state / coef_b) - jnp.abs(new_rate)
    )
    return (new_rate, new_state)


def real_rows(piece, total):
    sources, rows, chunk = piece.shape
    outer = total // INNER
    part = piece.reshape(sources, rows, chunk // INNER, INNER)
    table = jnp.stack(grid_tables(outer, outer, outer, -1.0), 1)
    table = table.reshape(sources, chunk // INNER, 2, outer)
    first = product("zrab,zakc->krcb", part, table)
    twist_re, twist_im = grid_tables(outer, INNER, total, -1.0)
    first = jnp.concatenate(twist(first[0], first[1], twist_re, twist_im), -1)
    second = complex_table(INNER, -1.0, 1.0 / math.sqrt(total))
    second = second.reshape(2 * INNER, 2, INNER)
    return [
        product("rcb,bm->mcr", first, second[:, part]).reshape(total, rows) for part in range(2)
    ]


def band_rows(part_re, part_im, sign):
    rows, total = part_re.shape
    outer = total // INNER
    table = complex_table(outer, sign).reshape(2 * outer, 2, outer)
    both = jnp.concatenate(
        [part_re.reshape(rows, outer, INNER), part_im.reshape(rows, outer, INNER)], 1
    )
    first = product("rab,akc->krcb", both, table)
    twist_re, twist_im = grid_tables(outer, INNER, total, sign)
    first = jnp.concatenate(twist(first[0], first[1], twist_re, twist_im), -1)
    second = complex_table(INNER, sign, 1.0 / math.sqrt(total)).reshape(2 * INNER, 2, INNER)
    return [
        product("rcb,bm->rmc", first, second[:, part]).reshape(rows, total) for part in range(2)
    ]


def real_cols(part_re, part_im):
    total, rows = part_re.shape
    outer = total // INNER
    both = jnp.concatenate(
        [part_re.reshape(outer, INNER, rows), part_im.reshape(outer, INNER, rows)], 0
    )
    table = complex_table(outer, 1.0).reshape(2 * outer, 2, outer)
    first = product("abr,akc->kcbr", both, table)
    twist_re, twist_im = grid_tables(outer, INNER, total, 1.0)
    first = jnp.concatenate(
        twist(first[0], first[1], twist_re[:, :, None], twist_im[:, :, None]), 1
    )
    second = complex_table(INNER, 1.0, 1.0 / math.sqrt(total)).reshape(2 * INNER, 2, INNER)
    return product("cbr,bm->rmc", first, second[:, 0]).reshape(rows, total)


def per_device(
    slip,
    slip_rate,
    state,
    loading,
    normal_stress,
    patch,
    rate_coef,
    state_coef,
    slip_scale,
    kernel,
    history,
):
    strike_count = lax.axis_size("strike")
    dip_count = lax.axis_size("dip")
    count = strike_count * dip_count
    both_axes = ("strike", "dip")
    cells_x, cells_y = slip.shape
    band, total_x = kernel.shape[1:]
    total_y = cells_y * dip_count
    rows = cells_x // dip_count
    keep = band // 2 + 1

    def gather_rows(array):
        return lax.all_to_all(
            array.reshape(dip_count, rows, cells_y), "dip", split_axis=0, concat_axis=0, tiled=True
        )

    def to_bands(part):
        return lax.all_to_all(part, both_axes, split_axis=0, concat_axis=1, tiled=True)

    slip_parts = real_rows(gather_rows(slip), total_y)
    rate_parts = real_rows(gather_rows(slip_rate), total_y)
    slip_parts = [part.reshape(count, band, rows)[:, :keep] for part in slip_parts]
    slip_both = jnp.concatenate(slip_parts, 1).reshape(count * 2 * keep, rows)
    slip_both = to_bands(slip_both)
    rate_parts = [to_bands(part) for part in rate_parts]
    slip_re, slip_im = band_rows(slip_both[:keep], slip_both[keep:], -1.0)
    rate_re, rate_im = band_rows(rate_parts[0], rate_parts[1], -1.0)
    rate_modes = jnp.stack([rate_re, rate_im]).astype(jnp.bfloat16)
    offset = (lax.axis_index("strike") * dip_count + lax.axis_index("dip")) * band
    row_index = lax.broadcasted_iota(jnp.int32, (keep,), 0)
    wave_y = wavenumber(offset + row_index, total_y)
    wave_x = wavenumber(lax.broadcasted_iota(jnp.int32, (total_x,), 0), total_x)
    magnitude = jnp.sqrt(wave_y[:, None] ** 2 + wave_x[None, :] ** 2)
    times = jnp.where((row_index == 0) | (row_index == band // 2), 1.0, 2.0)
    static = -0.5 * shear_modulus * magnitude * times[:, None]
    memory_re = jnp.einsum("jrc,jrc->rc", kernel, history[:, 0], preferred_element_type=jnp.float32)
    memory_im = jnp.einsum("jrc,jrc->rc", kernel, history[:, 1], preferred_element_type=jnp.float32)
    fill = ((0, band - keep), (0, 0))
    stress_re = jnp.pad(static * slip_re, fill) + memory_re
    stress_im = jnp.pad(static * slip_im, fill) + memory_im
    back = [
        lax.all_to_all(part, both_axes, split_axis=1, concat_axis=0, tiled=True)
        for part in band_rows(stress_re, stress_im, 1.0)
    ]
    line = real_cols(back[0], back[1])
    transfer = lax.all_to_all(line, "dip", split_axis=1, concat_axis=0, tiled=True)
    coef_a = lookup(patch, rate_coef)
    coef_b = lookup(patch, state_coef)
    length_l = lookup(patch, slip_scale)
    new_rate, new_state = friction(
        slip_rate, state, loading, normal_stress, transfer, coef_a, coef_b, length_l
    )
    return (new_rate, new_state, transfer, rate_modes)


def solution(mesh):
    return jax.shard_map(
        per_device,
        mesh=mesh,
        in_specs=(
            P("strike", "dip"),
            P("strike", "dip"),
            P("strike", "dip"),
            P("strike", "dip"),
            P("strike", "dip"),
            P("strike", "dip"),
            P(),
            P(),
            P(),
            P(None, ("strike", "dip"), None),
            P(None, None, ("strike", "dip"), None),
        ),
        out_specs=(
            P("strike", "dip"),
            P("strike", "dip"),
            P("strike", "dip"),
            P(None, ("strike", "dip"), None),
        ),
        check_vma=False,
    )
```

time: 590 us -> 537 us (0.910)
  matrix products: 137 us -> 55.9 us
  waiting for transfers between devices: 173 us -> 214 us
  local copies, waits for them, and re-layouts: 105 us -> 95.2 us
  starting transfers between devices: 41.4 us -> 32.8 us
  other arithmetic: 69.7 us -> 77.8 us
    dot_general x42 -> x17, matrix products: 137 us -> 55.9 us  [product(): return jnp.einsum(pattern, left_op, right_op, precision=lax.Precision.HIGH)]
    mul x19 -> x0, local copies, waits for them, and re-layouts: 62.6 us -> none  [the longest x9 30.5 us: transform_rows(): part_im.reshape(out_shape) * factor]
    all_to_all x8 -> x7, waiting for transfers between devices: 173 us -> 214 us  [the longest x2 74.5 us: per_device(): lax.all_to_all(part, both_axes, split_axis=1, concat_axis=0, tiled=True)]
    transpose x0 -> x11, local copies, waits for them, and re-layouts: none -> 25.1 us  [product(): return jnp.einsum(pattern, left_op, right_op, precision=lax.Precision.HIGH)]
    add x1, other arithmetic: 40.4 us -> 28.5 us  [friction(): state + time_step * (coef_b / length_l) * (jnp.exp(-state / coef_b) - jnp...]
    all_to_all x8 -> x7, starting transfers between devices: 41.4 us -> 32.8 us  [the longest x3 13.9 us: to_bands(): lax.all_to_all(part, both_axes, split_axis=0, concat_axis=1, tiled=True)]
    reshape x6 -> x14, local copies, waits for them, and re-layouts: 12 us -> 20.2 us  [the longest x2 5.7 us: real_rows(): part = piece.reshape(sources, rows, chunk // INNER, INNER)]
    another operation x0 -> x5, local copies, waits for them, and re-layouts: none -> 7.56 us  [the longest x2 5.8 us: per_device(): rate_modes = jnp.stack([rate_re, rate_im]).astype(jnp.bfloat16)]
  transfers between devices with their start and end apart: 8 -> 7, of which waited for: 6 -> 7; matrix products, arithmetic and copies ran while one was open for 39% -> 22% of each run, Pallas kernels for 0% -> 0%
where the time goes in v1:
time: 537 us; the launch traced here: 532 us
  waiting for transfers between devices  214 us (40%)
  local copies, waits for them, and re-layouts  95.2 us (18%)
  other arithmetic  77.8 us (14%)
  matrix products  55.9 us (10%)
  blocking collectives  54.6 us (10%)
  starting transfers between devices  32.8 us (6%)
    all_to_all x2, waiting for transfers between devices, per_device(): lax.all_to_all(part, both_axes, split_axis=1, concat_axis=0, tiled=True)  74.5 us
    all_to_all x3, waiting for transfers between devices, to_bands(): lax.all_to_all(part, both_axes, split_axis=0, concat_axis=1, tiled=True)  74.1 us
    dot_general x17, matrix products, product(): return jnp.einsum(pattern, left_op, right_op, precision=lax.Precision.HIGH)  55.9 us
    all_to_all x1, blocking collectives, gather_rows(): lax.all_to_all(array.reshape(dip_count, rows, cells_y), 'dip', split_axis...  54.6 us
    all_to_all x1, waiting for transfers between devices, gather_rows(): lax.all_to_all(array.reshape(dip_count, rows, cells_y), 'dip', split_axis...  41 us
    add x1, other arithmetic, friction(): state + time_step * (coef_b / length_l) * (jnp.exp(-state / coef_b) - jnp...  28.5 us
    transpose x11, local copies, waits for them, and re-layouts, product(): return jnp.einsum(pattern, left_op, right_op, precision=lax.Precision.HIGH)  25.1 us
    all_to_all x1, waiting for transfers between devices, per_device(): lax.all_to_all(line, 'dip', split_axis=1, concat_axis=0, tiled=True)  24.8 us
  transfers between devices with their start and end apart: 7, of which 7 were waited for; matrix products, arithmetic and copies ran while one was open for 22% of the time, Pallas kernels for 0%

profile of v1, /device:TPU:0, one launch (start us, length us, event | category | flops | bytes accessed | tf_op | source)
XLA Modules:
  0.0 532.2 jit_solution(14281215207955723238)
XLA Ops:
  0.6 54.6 %all_to_all.106 = f32[4,256,512]{2,1,0:T(8,128)S(1)} all-to-all(f32[4,256,512]{2,1,0:T(8,128)} %bitcast.293), channel_id=1, replica_groups=mesh['strike'=8,'dip'=4] {'dip'}, dimensions={0} | all-to-all | bytes 4194304 | tf_op jit(solution)/shard_map/all_to_all | solution.py:157
  55.2 4.5 all-to-all-start
  66.2 41.0 %all-to-all-done = f32[4,256,512]{2,1,0:T(8,128)} async-done(((f32[4,256,512]{2,1,0:T(8,128)}), f32[4,256,512]{2,1,0:T(8,128)}, u32[]{:S(2)}, u32[]{:S(2)}) %all-to-all-start) | async-done | bytes 2097184 | tf_op jit(solution)/shard_map/all_to_all | solution.py:157
  121.2 4.2 fusion.46
  128.0 4.1 all-to-all-start.6
  132.1 6.4 %fusion.49 = f32[128,16,256]{2,0,1:T(8,128)S(1)} fusion(f32[256,16,256]{2,1,0:T(8,128)} %copy-done, f32[256,2,128]{0,2,1:T(8,128)S(1)} %reshape.567), kind=kOutput, calls=%fused_computation.87 | convolution fusion | flops 805306368 | bytes 6422528 | tf_op jit(solution)/shard_map/rcb,bm->mcr/dot_general | solution.py:42
  141.0 38.0 %all-to-all-done.6 = f32[32,64,256]{2,1,0:T(8,128)S(1)} async-done(((f32[32,64,256]{2,1,0:T(8,128)}), f32[32,64,256]{2,1,0:T(8,128)S(1)}, u32[]{:S(2)}, u32[]{:S(2)}) %all-to-all-start.6) | async-done | bytes 2097184 | tf_op jit(solution)/shard_map/all_to_all | solution.py:162
  180.3 4.7 all-to-all-start.7
  188.8 4.2 fusion.40
  194.4 4.2 fusion.43
  201.6 30.1 %all-to-all-done.7 = f32[32,64,256]{2,1,0:T(8,128)} async-done(((f32[32,64,256]{2,1,0:T(8,128)}), f32[32,64,256]{2,1,0:T(8,128)}, u32[]{:S(2)}, u32[]{:S(2)}) %all-to-all-start.7) | async-done | bytes 2097184 | tf_op jit(solution)/shard_map/all_to_all | solution.py:162
  231.7 5.1 all-to-all-start.1
  243.8 20.0 %fusion = (f32[64,8192]{1,0:T(8,128)}, f32[64,8192]{1,0:T(8,128)}) fusion(bf16[16,64,8192]{2,1,0:T(8,128)(2,1)} %param.20, bf16[16,2,64,8192]{3,2,1,0:T(8,128)(2,1)} %param.21), kind=kLoop, calls=%fused_computation.2 | loop fusion | flops 57671680 | bytes 54525952 | tf_op jit(solution)/shard_map/jrc,jrc->rc/dot_general | solution.py:180
  263.9 4.1 copy.134
  270.6 4.1 copy.137
  277.5 6.1 %fusion.28 = f32[2,64,64,128]{3,2,1,0:T(8,128)} fusion(f32[64,64,128]{2,1,0:T(8,128)} %reshape.581, f32[64,64,128]{2,1,0:T(8,128)} %reshape.580, f32[128,2,64,1]{0,2,1,3:T(8,128)S(1)} %reshape.587), kind=kOutput, calls=%fused_computation.43 | convolution fusion | flops 806354944 | bytes 8454144 | tf_op jit(solution)/shard_map/rab,akc->krcb/dot_general | solution.py:42
  283.6 6.1 %all-to-all-done.1 = f32[32,66,256]{2,1,0:T(8,128)S(1)} async-done(((f32[32,66,256]{2,1,0:T(8,128)}), f32[32,66,256]{2,1,0:T(8,128)S(1)}, u32[]{:S(2)}, u32[]{:S(2)}) %all-to-all-start.1) | async-done | bytes 2162720 | tf_op jit(solution)/shard_map/all_to_all | solution.py:162
  319.1 3.8 copy.119
  322.9 4.8 all_to_all.81
  327.7 4.2 copy.120
  331.9 4.5 all-to-all-start.2
  336.4 4.7 fusion.39
  341.1 3.8 copy.121
  351.0 32.3 %all-to-all-done.2 = f32[64,32,256]{2,0,1:T(8,128)} async-done(((f32[64,32,256]{2,0,1:T(8,128)}), f32[64,32,256]{2,0,1:T(8,128)}, u32[]{:S(2)}, u32[]{:S(2)}) %all-to-all-start.2) | async-done | bytes 2097184 | tf_op jit(solution)/shard_map/all_to_all | solution.py:186
  383.3 4.7 all-to-all-start.3
  388.6 4.1 copy.123
  392.7 42.2 %all-to-all-done.3 = f32[64,32,256]{2,0,1:T(8,128)S(1)} async-done(((f32[64,32,256]{2,0,1:T(8,128)}), f32[64,32,256]{2,0,1:T(8,128)S(1)}, u32[]{:S(2)}, u32[]{:S(2)}) %all-to-all-start.3) | async-done | bytes 2097184 | tf_op jit(solution)/shard_map/all_to_all | solution.py:186
  445.8 5.2 all-to-all-start.4
  453.1 4.0 broadcast_compare_fusion
  464.0 4.4 fusion.59
  475.6 24.8 %all-to-all-done.4 = f32[256,4,512]{0,2,1:T(8,128)} async-done(((f32[256,4,512]{0,2,1:T(8,128)}), f32[256,4,512]{0,2,1:T(8,128)}, u32[]{:S(2)}, u32[]{:S(2)}) %all-to-all-start.4) | async-done | bytes 2097184 | tf_op jit(solution)/shard_map/all_to_all | solution.py:190
  503.5 28.5 %multiply_add_fusion.2 = (f32[1024,512]{1,0:T(8,128)}, f32[1024,512]{1,0:T(8,128)}) fusion(f32[1024,512]{1,0:T(8,128)} %param.13, pred[1024,512]{1,0:T(8,128)(4,1)} %get-tuple-element.24, pred[1024,512]{1,0:T(8,128)(4,1)S(1)} %copy-done.18, pred[1024,512]{1,0:T(8,128)(4,1)} %get-tuple-element.25, pred[1024,512]{1,0:T(8,128)(4,1)S(1)} %copy-done.17, ...), kind=kLoop, calls=%fused_computation.67 | loop fusion | flops 82837504 | bytes 16777264 | tf_op jit(solution)/shard_map/add | solution.py:79
  (154 shorter events, 113.2 us)
Async XLA Ops:
  55.2 51.9 %all-to-all-start = ((f32[4,256,512]{2,1,0:T(8,128)}), f32[4,256,512]{2,1,0:T(8,128)}, u32[]{:S(2)}, u32[]{:S(2)}) async-start(f32[4,256,512]{2,1,0:T(8,128)} %bitcast.292), calls=%async_computation | async-start | bytes 4194304 | tf_op jit(solution)/shard_map/all_to_all | solution.py:157
  113.2 2.4 copy-start.5
  121.2 4.3 copy-start
  128.0 51.0 %all-to-all-start.6 = ((f32[32,64,256]{2,1,0:T(8,128)}), f32[32,64,256]{2,1,0:T(8,128)S(1)}, u32[]{:S(2)}, u32[]{:S(2)}) async-start(f32[32,64,256]{2,1,0:T(8,128)} %bitcast.281), calls=%async_computation.6 | async-start | bytes 4194304 | tf_op jit(solution)/shard_map/all_to_all | solution.py:162
  179.0 1.3 copy-start.6
  180.3 51.4 %all-to-all-start.7 = ((f32[32,64,256]{2,1,0:T(8,128)}), f32[32,64,256]{2,1,0:T(8,128)}, u32[]{:S(2)}, u32[]{:S(2)}) async-start(f32[32,64,256]{2,1,0:T(8,128)} %bitcast.279), calls=%async_computation.7 | async-start | bytes 4194304 | tf_op jit(solution)/shard_map/all_to_all | solution.py:162
  231.7 58.0 %all-to-all-start.1 = ((f32[32,66,256]{2,1,0:T(8,128)}), f32[32,66,256]{2,1,0:T(8,128)S(1)}, u32[]{:S(2)}, u32[]{:S(2)}) async-start(f32[32,66,256]{2,1,0:T(8,128)} %pad_maximum_fusion.9), calls=%async_computation.1 | async-start | bytes 4718592 | tf_op jit(solution)/shard_map/all_to_all | solution.py:162
  291.0 1.3 copy-start.10
  302.3 1.8 copy-start.25
  304.1 2.0 copy-start.9
  306.3 1.6 copy-start.8
  309.0 2.2 copy-start.4
  309.0 2.2 copy-start.20
  309.0 2.2 copy-start.22
  309.0 2.2 copy-start.24
  311.2 4.6 copy-start.14
  314.5 1.3 copy-start.1
  331.9 51.4 %all-to-all-start.2 = ((f32[64,32,256]{2,0,1:T(8,128)}), f32[64,32,256]{2,0,1:T(8,128)}, u32[]{:S(2)}, u32[]{:S(2)}) async-start(f32[64,32,256]{2,0,1:T(8,128)} %copy.120), calls=%async_computation.2 | async-start | bytes 4194304 | tf_op jit(solution)/shard_map/all_to_all | solution.py:186
  351.0 37.6 %copy-start.15 = (f32[1,128,2,128]{1,3,2,0:T(8,128)S(1)}, f32[1,128,2,128]{1,3,2,0:T(8,128)}, u32[]{:S(2)}) copy-start(f32[1,128,2,128]{1,3,2,0:T(8,128)} %get-tuple-element.26) | copy-start | bytes 393220
  351.0 37.6 %copy-start.16 = (f32[1,128,2,128]{1,3,2,0:T(8,128)S(1)}, f32[1,128,2,128]{1,3,2,0:T(8,128)}, u32[]{:S(2)}) copy-start(f32[1,128,2,128]{1,3,2,0:T(8,128)} %get-tuple-element.29) | copy-start | bytes 393220
  383.3 51.6 %all-to-all-start.3 = ((f32[64,32,256]{2,0,1:T(8,128)}), f32[64,32,256]{2,0,1:T(8,128)S(1)}, u32[]{:S(2)}, u32[]{:S(2)}) async-start(f32[64,32,256]{2,0,1:T(8,128)} %copy.122), calls=%async_computation.3 | async-start | bytes 4194304 | tf_op jit(solution)/shard_map/all_to_all | solution.py:186
  434.9 1.6 copy-start.7
  445.8 5.3 copy-start.26
  445.8 5.9 %copy-start.27 = (f32[4]{0:T(128)S(1)}, f32[4]{0:T(128)}, u32[]{:S(2)}) copy-start(f32[4]{0:T(128)} %param.18) | copy-start | bytes 52
  445.8 6.6 %copy-start.28 = (f32[4]{0:T(128)S(1)}, f32[4]{0:T(128)}, u32[]{:S(2)}) copy-start(f32[4]{0:T(128)} %param.19) | copy-start | bytes 52
  445.8 11.2 %copy-start.12 = (f32[2,128,2,128]{3,1,0,2:T(8,128)S(1)}, f32[2,128,2,128]{3,1,0,2:T(8,128)}, u32[]{:S(2)}) copy-start(f32[2,128,2,128]{3,1,0,2:T(8,128)} %copy.106) | copy-start | bytes 786436
  445.8 54.7 %all-to-all-start.4 = ((f32[256,4,512]{0,2,1:T(8,128)}), f32[256,4,512]{0,2,1:T(8,128)}, u32[]{:S(2)}, u32[]{:S(2)}) async-start(f32[256,4,512]{0,2,1:T(8,128)} %bitcast.84), calls=%async_computation.4 | async-start | bytes 4194304 | tf_op jit(solution)/shard_map/all_to_all | solution.py:190
  453.0 4.0 copy-start.2
  453.0 4.0 copy-start.3
  500.5 3.0 copy-start.13
  500.5 3.0 copy-start.17
  500.5 3.0 copy-start.18
  (4 other events, 3.9 us)

commit v2 on v1

--- a/solution.py
+++ b/solution.py
@@ -1,8 +1,11 @@
+import functools
 import math
 
 import jax
 import jax.numpy as jnp
 from jax import lax
+from jax.experimental import pallas as pl
+from jax.experimental.pallas import tpu as pltpu
 from jax.sharding import PartitionSpec as P
 
 NEWTON = 8
@@ -56,18 +59,38 @@
     return 2.0 * math.pi / count * ((index + count // 2) % count - count // 2).astype(jnp.float32)
 
 
-def lookup(patch, table):
-    result = jnp.zeros(patch.shape, jnp.float32)
-    for label in range(table.shape[0]):
-        result = jnp.where(patch == label, table[label], result)
-    return result
-
-
-def friction(slip_rate, state, loading, normal_stress, transfer, coef_a, coef_b, length_l):
-    stress = loading + transfer
+def friction_kernel(
+    labels,
+    filled,
+    rate_coef,
+    state_coef,
+    slip_scale,
+    transfer_in,
+    slip_rate_in,
+    state_in,
+    loading_in,
+    normal_in,
+    patch_in,
+    *refs,
+):
+    new_rate_out, new_state_out, transfer_out = refs[filled:]
+    patch = patch_in[...]
+
+    def choose(table):
+        result = jnp.zeros(patch.shape, jnp.float32)
+        for label in range(labels):
+            result = jnp.where(patch == label, table[label], result)
+        return result
+
+    coef_a = choose(rate_coef)
+    coef_b = choose(state_coef)
+    length_l = choose(slip_scale)
+    transfer = transfer_in[0]
+    state = state_in[...]
+    stress = loading_in[...] + transfer
     prefix = 2.0 * jnp.exp(-state / coef_a)
-    angle_w = inverse_sinh(slip_rate / prefix)
-    weight = normal_stress * coef_a
+    angle_w = inverse_sinh(slip_rate_in[...] / prefix)
+    weight = normal_in[...] * coef_a
     half = 0.5 * damping * prefix
     for iteration in range(NEWTON):
         grow = half * jnp.exp(angle_w)
@@ -75,11 +98,35 @@
         residue = weight * angle_w + (grow - decay) - stress
         slope = weight + (grow + decay)
         angle_w = angle_w - relaxation * residue / (slope + jnp.abs(residue))
-    new_rate = prefix * jnp.sinh(angle_w)
-    new_state = state + time_step * (coef_b / length_l) * (
+    new_rate = (0.5 * prefix) * (jnp.exp(angle_w) - jnp.exp(-angle_w))
+    new_rate_out[...] = new_rate
+    new_state_out[...] = state + time_step * (coef_b / length_l) * (
         jnp.exp(-state / coef_b) - jnp.abs(new_rate)
     )
-    return (new_rate, new_state)
+    transfer_out[...] = transfer
+
+
+def friction(part, parts, tables, transfer, cells, before):
+    sources, rows, columns = transfer.shape
+    block = pl.BlockSpec((rows, columns), lambda step: (step * parts + part, 0))
+    scalar = pl.BlockSpec(memory_space=pltpu.SMEM)
+    size = transfer.size
+    first = len(tables) + 1 + len(cells)
+    return pl.pallas_call(
+        functools.partial(friction_kernel, tables[0].shape[0], len(before)),
+        grid=(sources,),
+        out_shape=[jax.ShapeDtypeStruct(cells[0].shape, jnp.float32)] * 3,
+        in_specs=[scalar] * len(tables)
+        + [pl.BlockSpec((1, rows, columns), lambda step: (step, 0, 0))]
+        + [block] * len(cells)
+        + [pl.BlockSpec(memory_space=pl.ANY)] * len(before),
+        out_specs=[block] * 3,
+        input_output_aliases={first + index: index for index in range(len(before))},
+        compiler_params=pltpu.CompilerParams(vmem_limit_bytes=32 * 1024 * 1024),
+        cost_estimate=pl.CostEstimate(
+            flops=size * 200, bytes_accessed=size * 36, transcendentals=size * 30
+        ),
+    )(*tables, transfer, *cells, *before)
 
 
 def real_rows(piece, total):
@@ -161,15 +208,28 @@
     def to_bands(part):
         return lax.all_to_all(part, both_axes, split_axis=0, concat_axis=1, tiled=True)
 
-    slip_parts = real_rows(gather_rows(slip), total_y)
-    rate_parts = real_rows(gather_rows(slip_rate), total_y)
-    slip_parts = [part.reshape(count, band, rows)[:, :keep] for part in slip_parts]
-    slip_both = jnp.concatenate(slip_parts, 1).reshape(count * 2 * keep, rows)
+    def after(value, earlier):
+        return lax.optimization_barrier((value, earlier))
+
+    def band_piece(pair, start, stop):
+        pieces = [part.reshape(count, band, rows)[:, start:stop] for part in pair]
+        return jnp.concatenate(pieces, 1).reshape(count * 2 * (stop - start), rows)
+
+    def modes(piece):
+        half = piece.shape[0] // 2
+        return jnp.stack(band_rows(piece[:half], piece[half:], -1.0)).astype(jnp.bfloat16)
+
+    slip_rows = gather_rows(slip)
+    rate_rows, slip_rows = after(slip_rate, slip_rows)
+    rate_rows = gather_rows(rate_rows)
+    slip_parts = real_rows(slip_rows, total_y)
+    slip_both, rate_rows = after(band_piece(slip_parts, 0, keep), rate_rows)
     slip_both = to_bands(slip_both)
-    rate_parts = [to_bands(part) for part in rate_parts]
+    rate_parts = real_rows(rate_rows, total_y)
+    cut = band - band // 4
+    rate_first, slip_both = after(band_piece(rate_parts, 0, cut), slip_both)
+    rate_first = to_bands(rate_first)
     slip_re, slip_im = band_rows(slip_both[:keep], slip_both[keep:], -1.0)
-    rate_re, rate_im = band_rows(rate_parts[0], rate_parts[1], -1.0)
-    rate_modes = jnp.stack([rate_re, rate_im]).astype(jnp.bfloat16)
     offset = (lax.axis_index("strike") * dip_count + lax.axis_index("dip")) * band
     row_index = lax.broadcasted_iota(jnp.int32, (keep,), 0)
     wave_y = wavenumber(offset + row_index, total_y)
@@ -182,19 +242,34 @@
     fill = ((0, band - keep), (0, 0))
     stress_re = jnp.pad(static * slip_re, fill) + memory_re
     stress_im = jnp.pad(static * slip_im, fill) + memory_im
-    back = [
-        lax.all_to_all(part, both_axes, split_axis=1, concat_axis=0, tiled=True)
-        for part in band_rows(stress_re, stress_im, 1.0)
-    ]
-    line = real_cols(back[0], back[1])
-    transfer = lax.all_to_all(line, "dip", split_axis=1, concat_axis=0, tiled=True)
-    coef_a = lookup(patch, rate_coef)
-    coef_b = lookup(patch, state_coef)
-    length_l = lookup(patch, slip_scale)
-    new_rate, new_state = friction(
-        slip_rate, state, loading, normal_stress, transfer, coef_a, coef_b, length_l
-    )
-    return (new_rate, new_state, transfer, rate_modes)
+    back_parts = band_rows(stress_re, stress_im, 1.0)
+
+    back = jnp.concatenate(back_parts, 0)
+    back, rate_first = after(back, rate_first)
+    back = lax.all_to_all(back, both_axes, split_axis=1, concat_axis=0, tiled=True)
+    modes_first = modes(rate_first)
+    rate_last, (back, modes_first) = after(
+        band_piece(rate_parts, cut, band), (back, modes_first)
+    )
+    rate_last = to_bands(rate_last)
+    back = back.reshape(count, 2, band, rows)
+    line = real_cols(back[:, 0].reshape(total_y, rows), back[:, 1].reshape(total_y, rows))
+    line, rate_last = after(line, rate_last)
+    tables = (rate_coef, state_coef, slip_scale)
+    cells = (slip_rate, state, loading, normal_stress, patch)
+    parts = 2
+    pieces = []
+    for part in range(parts):
+        piece = line[part * (rows // parts) : (part + 1) * (rows // parts)]
+        piece = piece.reshape(rows // parts, dip_count, cells_y).transpose(1, 0, 2)
+        if pieces:
+            piece, pieces[-1] = after(piece, pieces[-1])
+        pieces.append(lax.all_to_all(piece, "dip", split_axis=0, concat_axis=0, tiled=True))
+    rate_modes = jnp.concatenate([modes_first, modes(rate_last)], 1)
+    outs = []
+    for part in range(parts):
+        outs = friction(part, parts, tables, pieces[part], cells, outs)
+    return (*outs, rate_modes)
 
 
 def solution(mesh):

time: 537 us -> 466 us (0.87)
  blocking collectives: 54.6 us -> 0 us
  other arithmetic: 77.8 us -> 44.5 us
  Pallas kernels: 0 us -> 20.7 us
  waiting for transfers between devices: 214 us -> 202 us
  local copies, waits for them, and re-layouts: 95.2 us -> 102 us
    all_to_all x1 -> x0, blocking collectives: 54.6 us -> none  [gather_rows(): lax.all_to_all(array.reshape(dip_count, rows, cells_y), 'dip', split_axis...]
    all_to_all x3, waiting for transfers between devices: 74.1 us -> 35.9 us  [to_bands(): lax.all_to_all(part, both_axes, split_axis=0, concat_axis=1, tiled=True)]
    add x1 -> x0, other arithmetic: 28.5 us -> none  [friction(): state + time_step * (coef_b / length_l) * (jnp.exp(-state / coef_b) - jnp...]
    all_to_all x1 -> x2, waiting for transfers between devices: 41 us -> 67.6 us  [gather_rows(): lax.all_to_all(array.reshape(dip_count, rows, cells_y), 'dip', split_axis...]
    pallas_call x0 -> x2, Pallas kernels: none -> 20.7 us  [friction(): pl.pallas_call(functools.partial(friction_kernel, tables[0].shape[0], len...]
    all_to_all x7 -> x1, local copies, waits for them, and re-layouts: 22.7 us -> 2.56 us  [per_device(): lax.all_to_all(back, both_axes, split_axis=1, concat_axis=0, tiled=True)]
    unnamed x60 -> x82, local copies, waits for them, and re-layouts: 6.89 us -> 20.3 us
    reshape x2 -> x4, local copies, waits for them, and re-layouts: 2.47 us -> 14.1 us  [band_rows(): product('rcb,bm->rmc', first, second[:, part]).reshape(rows, total)]
  transfers between devices with their start and end apart: 7 -> 8, of which waited for: 7 -> 8; matrix products, arithmetic and copies ran while one was open for 22% -> 36% of each run, Pallas kernels for 0% -> 2%
where the time goes in v2:
time: 466 us; the launch traced here: 460 us
  waiting for transfers between devices  202 us (43%)
  local copies, waits for them, and re-layouts  102 us (22%)
  matrix products  51 us (11%)
  other arithmetic  44.5 us (10%)
  starting transfers between devices  38.1 us (8%)
  Pallas kernels  20.7 us (4%)
    all_to_all x1, waiting for transfers between devices, per_device(): lax.all_to_all(back, both_axes, split_axis=1, concat_axis=0, tiled=True)  69.5 us
    all_to_all x2, waiting for transfers between devices, gather_rows(): lax.all_to_all(array.reshape(dip_count, rows, cells_y), 'dip', split_axis...  67.6 us
    dot_general x20, matrix products, product(): return jnp.einsum(pattern, left_op, right_op, precision=lax.Precision.HIGH)  51 us
    all_to_all x3, waiting for transfers between devices, to_bands(): lax.all_to_all(part, both_axes, split_axis=0, concat_axis=1, tiled=True)  35.9 us
    all_to_all x2, waiting for transfers between devices, per_device(): lax.all_to_all(piece, 'dip', split_axis=0, concat_axis=0, tiled=True)  28.8 us
    transpose x13, local copies, waits for them, and re-layouts, product(): return jnp.einsum(pattern, left_op, right_op, precision=lax.Precision.HIGH)  23.5 us
    pallas_call x2, Pallas kernels, friction(): pl.pallas_call(functools.partial(friction_kernel, tables[0].shape[0], len...  20.7 us
    unnamed x82, local copies, waits for them, and re-layouts  20.3 us
  transfers between devices with their start and end apart: 8, of which 8 were waited for; matrix products, arithmetic and copies ran while one was open for 36% of the time, Pallas kernels for 2%

profile of v2, /device:TPU:0, one launch (start us, length us, event | category | flops | bytes accessed | tf_op | source)
XLA Modules:
  0.0 459.5 jit_solution(2088597446656322348)
XLA Ops:
  0.6 6.4 %all-to-all-start = ((f32[4,256,512]{2,1,0:T(8,128)}), f32[4,256,512]{2,1,0:T(8,128)S(1)}, u32[]{:S(2)}, u32[]{:S(2)}) async-start(f32[4,256,512]{2,1,0:T(8,128)} %bitcast.363), calls=%async_computation | async-start | bytes 4194304 | tf_op jit(solution)/shard_map/all_to_all | solution.py:204
  9.7 45.5 %all-to-all-done = f32[4,256,512]{2,1,0:T(8,128)S(1)} async-done(((f32[4,256,512]{2,1,0:T(8,128)}), f32[4,256,512]{2,1,0:T(8,128)S(1)}, u32[]{:S(2)}, u32[]{:S(2)}) %all-to-all-start) | async-done | bytes 2097184 | tf_op jit(solution)/shard_map/all_to_all | solution.py:204
  55.2 4.5 all-to-all-start.1
  72.1 4.2 fusion.37
  77.7 4.2 fusion.40
  85.4 22.1 %all-to-all-done.1 = f32[4,256,512]{2,1,0:T(8,128)} async-done(((f32[4,256,512]{2,1,0:T(8,128)}), f32[4,256,512]{2,1,0:T(8,128)}, u32[]{:S(2)}, u32[]{:S(2)}) %all-to-all-start.1) | async-done | bytes 2097184 | tf_op jit(solution)/shard_map/all_to_all | solution.py:204
  110.3 3.7 all-to-all-start.2
  114.0 20.0 %fusion = (f32[64,8192]{1,0:T(8,128)}, f32[64,8192]{1,0:T(8,128)}) fusion(bf16[16,64,8192]{2,1,0:T(8,128)(2,1)} %param.20, bf16[16,2,64,8192]{3,2,1,0:T(8,128)(2,1)} %param.21), kind=kLoop, calls=%fused_computation.2 | loop fusion | flops 57671680 | bytes 54525952 | tf_op jit(solution)/shard_map/jrc,jrc->rc/dot_general | solution.py:240
  139.9 3.7 convolution_bitcast_fusion
  144.4 4.2 fusion.43
  149.9 4.2 fusion.46
  159.1 7.9 %all-to-all-done.2 = f32[32,66,256]{2,1,0:T(8,128)S(1)} async-done(((f32[32,66,256]{2,1,0:T(8,128)}), f32[32,66,256]{2,1,0:T(8,128)S(1)}, u32[]{:S(2)}, u32[]{:S(2)}) %all-to-all-start.2) | async-done | bytes 2162720 | tf_op jit(solution)/shard_map/all_to_all | solution.py:209
  169.5 4.4 all-to-all-start.3
  201.0 3.9 copy.90
  204.9 4.8 %reshape.584 = f32[64,8192]{1,0:T(8,128)} reshape(f32[64,128,64]{2,1,0:T(8,128)} %copy.90) | data formatting | bytes 4194304 | tf_op jit(solution)/shard_map/reshape | solution.py:160
  209.6 4.7 %fusion.36 = f32[64,128,64]{1,2,0:T(8,128)} fusion(f32[64,64,128]{2,1,0:T(8,128)} %copy-done.12, f32[64,64,128]{2,1,0:T(8,128)S(1)} %get-tuple-element.50, f32[256,2,128]{2,0,1:T(8,128)S(1)} %bitcast.367), kind=kOutput, calls=%fused_computation.73 | convolution fusion | flops 806354944 | bytes 6422528 | tf_op jit(solution)/shard_map/rcb,bm->rmc/dot_general | solution.py:45
  214.3 3.9 copy.91
  218.2 5.3 %reshape.585 = f32[64,8192]{1,0:T(8,128)} reshape(f32[64,128,64]{2,1,0:T(8,128)} %copy.91) | data formatting | bytes 4194304 | tf_op jit(solution)/shard_map/reshape | solution.py:160
  223.5 4.1 pad_maximum_fusion.3
  227.6 16.3 %all-to-all-done.3 = f32[32,96,256]{2,1,0:T(8,128)} async-done(((f32[32,96,256]{2,1,0:T(8,128)}), f32[32,96,256]{2,1,0:T(8,128)}, u32[]{:S(2)}, u32[]{:S(2)}) %all-to-all-start.3) | async-done | bytes 3145760 | tf_op jit(solution)/shard_map/all_to_all | solution.py:209
  249.6 5.0 %all-to-all-start.4 = ((f32[128,32,256]{2,0,1:T(8,128)}), f32[128,32,256]{2,0,1:T(8,128)}, u32[]{:S(2)}, u32[]{:S(2)}) async-start(f32[128,32,256]{2,0,1:T(8,128)} %bitcast.328), calls=%async_computation.4 | async-start | bytes 8388608 | tf_op jit(solution)/shard_map/all_to_all | solution.py:249
  267.3 3.2 stack_reshape.16
  277.2 69.5 %all-to-all-done.4 = f32[128,32,256]{2,0,1:T(8,128)} async-done(((f32[128,32,256]{2,0,1:T(8,128)}), f32[128,32,256]{2,0,1:T(8,128)}, u32[]{:S(2)}, u32[]{:S(2)}) %all-to-all-start.4) | async-done | bytes 4194336 | tf_op jit(solution)/shard_map/all_to_all | solution.py:249
  346.8 5.7 %all-to-all-start.5 = ((f32[32,32,256]{2,1,0:T(8,128)}), f32[32,32,256]{2,1,0:T(8,128)S(1)}, u32[]{:S(2)}, u32[]{:S(2)}) async-start(f32[32,32,256]{2,1,0:T(8,128)} %bitcast.106), calls=%async_computation.5 | async-start | bytes 2097152 | tf_op jit(solution)/shard_map/all_to_all | solution.py:209
  361.1 3.5 fusion.49
  365.8 11.6 %all-to-all-done.5 = f32[32,32,256]{2,1,0:T(8,128)S(1)} async-done(((f32[32,32,256]{2,1,0:T(8,128)}), f32[32,32,256]{2,1,0:T(8,128)S(1)}, u32[]{:S(2)}, u32[]{:S(2)}) %all-to-all-start.5) | async-done | bytes 1048608 | tf_op jit(solution)/shard_map/all_to_all | solution.py:209
  382.2 4.9 %all-to-all-start.6 = ((f32[4,128,512]{2,1,0:T(8,128)}), f32[4,128,512]{2,1,0:T(8,128)S(1)}, u32[]{:S(2)}, u32[]{:S(2)}) async-start(f32[4,128,512]{2,1,0:T(8,128)} %bitcast.111), calls=%async_computation.6 | async-start | bytes 2097152 | tf_op jit(solution)/shard_map/all_to_all | solution.py:267
  389.2 24.6 %all-to-all-done.6.transfer_in = f32[4,128,512]{2,1,0:T(8,128)S(1)} async-done(((f32[4,128,512]{2,1,0:T(8,128)}), f32[4,128,512]{2,1,0:T(8,128)S(1)}, u32[]{:S(2)}, u32[]{:S(2)}) %all-to-all-start.6) | async-done | bytes 1048608 | tf_op jit(solution)/shard_map/all_to_all | solution.py:267
  414.8 3.5 all-to-all-start.7
  429.6 10.3 %shard_map.138 = (f32[1024,512]{1,0:T(8,128)}, f32[1024,512]{1,0:T(8,128)}, f32[1024,512]{1,0:T(8,128)}) custom-call(f32[4]{0:T(128)S(1)} %copy-done.9, f32[4]{0:T(128)S(1)} %copy-done.10, f32[4]{0:T(128)S(1)} %copy-done.11, f32[4,128,512]{2,1,0:T(8,128)S(1)} %copy-done.8, f32[1024,512]{1,0:T(8,128)} %slip_rate_in.3, f32[1024,512]{1,0:T(8,128)S(1)} %copy-done, ...), custom_call_target="tpu_custom_call" | custom-call | flops 52428800 | bytes 9437184 | tf_op jit(solution)/shard_map/pallas_call | solution.py:115
  439.9 4.3 all-to-all-done.7.transfer_in
  448.9 10.3 %shard_map.139 = (f32[1024,512]{1,0:T(8,128)}, f32[1024,512]{1,0:T(8,128)}, f32[1024,512]{1,0:T(8,128)}) custom-call(f32[4]{0:T(128)S(1)} %copy-done.9, f32[4]{0:T(128)S(1)} %copy-done.10, f32[4]{0:T(128)S(1)} %copy-done.11, f32[4,128,512]{2,1,0:T(8,128)S(1)} %all-to-all-done.7.transfer_in, ...), custom_call_target="tpu_custom_call", output_to_operand_aliasing={{0}: (9, {}), {1}: (10, {}), {2}: (11, {})} | custom-call | flops 52428800 | bytes 9437184 | tf_op jit(solution)/shard_map/pallas_call | solution.py:115
  (193 shorter events, 123.1 us)
Async XLA Ops:
  0.6 54.6 %all-to-all-start = ((f32[4,256,512]{2,1,0:T(8,128)}), f32[4,256,512]{2,1,0:T(8,128)S(1)}, u32[]{:S(2)}, u32[]{:S(2)}) async-start(f32[4,256,512]{2,1,0:T(8,128)} %bitcast.363), calls=%async_computation | async-start | bytes 4194304 | tf_op jit(solution)/shard_map/all_to_all | solution.py:204
  55.2 52.3 %all-to-all-start.1 = ((f32[4,256,512]{2,1,0:T(8,128)}), f32[4,256,512]{2,1,0:T(8,128)}, u32[]{:S(2)}, u32[]{:S(2)}) async-start(f32[4,256,512]{2,1,0:T(8,128)} %bitcast.35), calls=%async_computation.1 | async-start | bytes 4194304 | tf_op jit(solution)/shard_map/all_to_all | solution.py:204
  60.9 113.9 %copy-start.23 = (f32[128,2,64,1]{0,2,1,3:T(8,128)}, f32[128,2,64,1]{0,2,1,3:T(8,128)S(1)}, u32[]{:S(2)}) copy-start(f32[128,2,64,1]{0,2,1,3:T(8,128)S(1)} %reshape.601) | copy-start | bytes 196612
  63.0 113.3 %copy-start.20 = (f32[2,128,2,128]{3,1,0,2:T(8,128)}, f32[2,128,2,128]{3,1,0,2:T(8,128)S(1)}, u32[]{:S(2)}) copy-start(f32[2,128,2,128]{3,1,0,2:T(8,128)S(1)} %copy.85) | copy-start | bytes 786436
  64.7 111.2 %copy-start.26 = (f32[64,128]{1,0:T(8,128)}, f32[64,128]{1,0:T(8,128)S(1)}, u32[]{:S(2)}) copy-start(f32[64,128]{1,0:T(8,128)S(1)} %get-tuple-element.100) | copy-start | bytes 98308
  110.3 56.7 %all-to-all-start.2 = ((f32[32,66,256]{2,1,0:T(8,128)}), f32[32,66,256]{2,1,0:T(8,128)S(1)}, u32[]{:S(2)}, u32[]{:S(2)}) async-start(f32[32,66,256]{2,1,0:T(8,128)} %all_to_all.70), calls=%async_computation.2 | async-start | bytes 4718592 | tf_op jit(solution)/shard_map/all_to_all | solution.py:209
  149.9 7.1 %copy-start.14 = (f32[128,16,256]{2,1,0:T(8,128)}, f32[128,16,256]{2,1,0:T(8,128)S(1)}, u32[]{:S(2)}) copy-start(f32[128,16,256]{2,1,0:T(8,128)S(1)} %copy.80) | copy-start | bytes 6291460
  169.5 74.4 %all-to-all-start.3 = ((f32[32,96,256]{2,1,0:T(8,128)}), f32[32,96,256]{2,1,0:T(8,128)}, u32[]{:S(2)}, u32[]{:S(2)}) async-start(f32[32,96,256]{2,1,0:T(8,128)} %bitcast.88), calls=%async_computation.3 | async-start | bytes 6291456 | tf_op jit(solution)/shard_map/all_to_all | solution.py:209
  186.8 1.8 copy-start.34
  188.6 2.0 copy-start.18
  190.8 1.6 copy-start.17
  193.5 2.0 copy-start.33
  195.5 2.3 copy-start.25
  218.2 5.3 %copy-start.16 = (f32[64,8192]{1,0:T(8,128)S(1)}, f32[64,8192]{1,0:T(8,128)}, u32[]{:S(2)}) copy-start(f32[64,8192]{1,0:T(8,128)} %reshape.584) | copy-start | bytes 6291460
  243.9 3.1 copy-start.13
  249.6 97.2 %all-to-all-start.4 = ((f32[128,32,256]{2,0,1:T(8,128)}), f32[128,32,256]{2,0,1:T(8,128)}, u32[]{:S(2)}, u32[]{:S(2)}) async-start(f32[128,32,256]{2,0,1:T(8,128)} %bitcast.328), calls=%async_computation.4 | async-start | bytes 8388608 | tf_op jit(solution)/shard_map/all_to_all | solution.py:249
  272.7 3.2 copy-start.22
  275.9 76.9 %copy-start.29 = (f32[1,128,2,128]{1,3,2,0:T(8,128)S(1)}, f32[1,128,2,128]{1,3,2,0:T(8,128)}, u32[]{:S(2)}) copy-start(f32[1,128,2,128]{1,3,2,0:T(8,128)} %get-tuple-element.72) | copy-start | bytes 393220
  275.9 76.9 %copy-start.30 = (f32[1,128,2,128]{1,3,2,0:T(8,128)S(1)}, f32[1,128,2,128]{1,3,2,0:T(8,128)}, u32[]{:S(2)}) copy-start(f32[1,128,2,128]{1,3,2,0:T(8,128)} %get-tuple-element.75) | copy-start | bytes 393220
  346.8 30.7 %all-to-all-start.5 = ((f32[32,32,256]{2,1,0:T(8,128)}), f32[32,32,256]{2,1,0:T(8,128)S(1)}, u32[]{:S(2)}, u32[]{:S(2)}) async-start(f32[32,32,256]{2,1,0:T(8,128)} %bitcast.106), calls=%async_computation.5 | async-start | bytes 2097152 | tf_op jit(solution)/shard_map/all_to_all | solution.py:209
  357.8 2.0 copy-start.32
  382.2 6.2 %copy-start.19 = (f32[32,4,8,256]{3,2,0,1:T(8,128)S(1)}, f32[32,4,8,256]{3,2,0,1:T(8,128)}, u32[]{:S(2)}) copy-start(f32[32,4,8,256]{3,2,0,1:T(8,128)} %copy.134) | copy-start | bytes 3145732
  382.2 31.6 %all-to-all-start.6 = ((f32[4,128,512]{2,1,0:T(8,128)}), f32[4,128,512]{2,1,0:T(8,128)S(1)}, u32[]{:S(2)}, u32[]{:S(2)}) async-start(f32[4,128,512]{2,1,0:T(8,128)} %bitcast.111), calls=%async_computation.6 | async-start | bytes 2097152 | tf_op jit(solution)/shard_map/all_to_all | solution.py:267
  389.2 29.1 %copy-start.28 = (f32[64,128]{1,0:T(8,128)S(1)}, f32[64,128]{1,0:T(8,128)}, u32[]{:S(2)}) copy-start(f32[64,128]{1,0:T(8,128)} %copy-done.26) | copy-start | bytes 98308
  414.8 29.4 %all-to-all-start.7 = ((f32[4,128,512]{2,1,0:T(8,128)}), f32[4,128,512]{2,1,0:T(8,128)S(1)}, u32[]{:S(2)}, u32[]{:S(2)}) async-start(f32[4,128,512]{2,1,0:T(8,128)} %bitcast.109), calls=%async_computation.7 | async-start | bytes 2097152 | tf_op jit(solution)/shard_map/all_to_all | solution.py:267
  418.5 6.7 %copy-start.9 = (f32[4]{0:T(128)S(1)}, f32[4]{0:T(128)}, u32[]{:S(2)}) copy-start(f32[4]{0:T(128)} %rate_coef.3) | copy-start | bytes 52
  418.5 6.6 %copy-start.10 = (f32[4]{0:T(128)S(1)}, f32[4]{0:T(128)}, u32[]{:S(2)}) copy-start(f32[4]{0:T(128)} %state_coef.3) | copy-start | bytes 52
  418.5 6.6 %copy-start.11 = (f32[4]{0:T(128)S(1)}, f32[4]{0:T(128)}, u32[]{:S(2)}) copy-start(f32[4]{0:T(128)} %slip_scale.3) | copy-start | bytes 52
  422.0 3.2 copy-start
  422.0 3.2 copy-start.1
  425.2 1.6 copy-start.3
  444.2 1.6 copy-start.2
  (11 other events, 13.8 us)

commit v3 on v2

--- a/solution.py
+++ b/solution.py
@@ -206,14 +206,15 @@
         )
 
     def to_bands(part):
-        return lax.all_to_all(part, both_axes, split_axis=0, concat_axis=1, tiled=True)
+        piece = lax.all_to_all(part, both_axes, split_axis=0, concat_axis=0, tiled=True)
+        return piece.transpose(1, 0, 2).reshape(piece.shape[1], count * rows)
 
     def after(value, earlier):
         return lax.optimization_barrier((value, earlier))
 
     def band_piece(pair, start, stop):
         pieces = [part.reshape(count, band, rows)[:, start:stop] for part in pair]
-        return jnp.concatenate(pieces, 1).reshape(count * 2 * (stop - start), rows)
+        return jnp.concatenate(pieces, 1)
 
     def modes(piece):
         half = piece.shape[0] // 2
@@ -244,9 +245,9 @@
     stress_im = jnp.pad(static * slip_im, fill) + memory_im
     back_parts = band_rows(stress_re, stress_im, 1.0)
 
-    back = jnp.concatenate(back_parts, 0)
+    back = jnp.concatenate(back_parts, 0).reshape(2 * band, count, rows).transpose(1, 0, 2)
     back, rate_first = after(back, rate_first)
-    back = lax.all_to_all(back, both_axes, split_axis=1, concat_axis=0, tiled=True)
+    back = lax.all_to_all(back, both_axes, split_axis=0, concat_axis=0, tiled=True)
     modes_first = modes(rate_first)
     rate_last, (back, modes_first) = after(
         band_piece(rate_parts, cut, band), (back, modes_first)

time: 466 us -> 465 us (level)
    concatenate x0 -> x2, local copies, waits for them, and re-layouts: none -> 10.2 us  [per_device(): jnp.concatenate(back_parts, 0).reshape(2 * band, count, rows)]
    reshape x4 -> x2, local copies, waits for them, and re-layouts: 14.1 us -> 4.07 us  [band_rows(): product('rcb,bm->rmc', first, second[:, part]).reshape(rows, total)]
    all_to_all x5 -> x0, local copies, waits for them, and re-layouts: 9.52 us -> none  [the longest x4 6.96 us: to_bands(): lax.all_to_all(part, both_axes, split_axis=0, concat_axis=1, tiled=True)]
where the time goes in v3:
time: 465 us; the launch traced here: 459 us
  waiting for transfers between devices  202 us (43%)
  local copies, waits for them, and re-layouts  99.2 us (21%)
  matrix products  51 us (11%)
  other arithmetic  46.1 us (10%)
  starting transfers between devices  38.1 us (8%)
  Pallas kernels  20.7 us (4%)
    all_to_all x1, waiting for transfers between devices, per_device(): lax.all_to_all(back, both_axes, split_axis=0, concat_axis=0, tiled=True)  69.5 us
    all_to_all x2, waiting for transfers between devices, gather_rows(): lax.all_to_all(array.reshape(dip_count, rows, cells_y), 'dip', split_axis...  67.6 us
    dot_general x20, matrix products, product(): return jnp.einsum(pattern, left_op, right_op, precision=lax.Precision.HIGH)  51 us
    all_to_all x3, waiting for transfers between devices, to_bands(): lax.all_to_all(part, both_axes, split_axis=0, concat_axis=0, tiled=True)  35.6 us
    all_to_all x2, waiting for transfers between devices, per_device(): lax.all_to_all(piece, 'dip', split_axis=0, concat_axis=0, tiled=True)  28.8 us
    transpose x13, local copies, waits for them, and re-layouts, product(): return jnp.einsum(pattern, left_op, right_op, precision=lax.Precision.HIGH)  23.5 us
    pallas_call x2, Pallas kernels, friction(): pl.pallas_call(functools.partial(friction_kernel, tables[0].shape[0], len...  20.7 us
    unnamed x82, local copies, waits for them, and re-layouts  20.3 us
  transfers between devices with their start and end apart: 8, of which 8 were waited for; matrix products, arithmetic and copies ran while one was open for 36% of the time, Pallas kernels for 2%

profile of v3, /device:TPU:0, one launch (start us, length us, event | category | flops | bytes accessed | tf_op | source)
XLA Modules:
  0.0 458.5 jit_solution(5594720712422980839)
XLA Ops:
  0.6 6.4 %all-to-all-start = ((f32[4,256,512]{2,1,0:T(8,128)}), f32[4,256,512]{2,1,0:T(8,128)S(1)}, u32[]{:S(2)}, u32[]{:S(2)}) async-start(f32[4,256,512]{2,1,0:T(8,128)} %bitcast.348), calls=%async_computation | async-start | bytes 4194304 | tf_op jit(solution)/shard_map/all_to_all | solution.py:204
  9.7 45.5 %all-to-all-done = f32[4,256,512]{2,1,0:T(8,128)S(1)} async-done(((f32[4,256,512]{2,1,0:T(8,128)}), f32[4,256,512]{2,1,0:T(8,128)S(1)}, u32[]{:S(2)}, u32[]{:S(2)}) %all-to-all-start) | async-done | bytes 2097184 | tf_op jit(solution)/shard_map/all_to_all | solution.py:204
  55.2 4.5 all-to-all-start.1
  72.1 4.2 fusion.37
  77.7 4.2 fusion.40
  85.4 22.1 %all-to-all-done.1 = f32[4,256,512]{2,1,0:T(8,128)} async-done(((f32[4,256,512]{2,1,0:T(8,128)}), f32[4,256,512]{2,1,0:T(8,128)}, u32[]{:S(2)}, u32[]{:S(2)}) %all-to-all-start.1) | async-done | bytes 2097184 | tf_op jit(solution)/shard_map/all_to_all | solution.py:204
  107.5 3.7 all-to-all-start.2
  111.2 20.0 %fusion = (f32[64,8192]{1,0:T(8,128)}, f32[64,8192]{1,0:T(8,128)}) fusion(bf16[16,64,8192]{2,1,0:T(8,128)(2,1)} %param.20, bf16[16,2,64,8192]{3,2,1,0:T(8,128)(2,1)} %param.21), kind=kLoop, calls=%fused_computation.2 | loop fusion | flops 57671680 | bytes 54525952 | tf_op jit(solution)/shard_map/jrc,jrc->rc/dot_general | solution.py:241
  137.1 3.7 convolution_bitcast_fusion
  141.6 4.2 fusion.43
  147.0 4.2 fusion.46
  156.3 7.9 %all-to-all-done.2 = f32[32,66,256]{2,1,0:T(8,128)S(1)} async-done(((f32[32,66,256]{2,1,0:T(8,128)}), f32[32,66,256]{2,1,0:T(8,128)S(1)}, u32[]{:S(2)}, u32[]{:S(2)}) %all-to-all-start.2) | async-done | bytes 2162720 | tf_op jit(solution)/shard_map/all_to_all | solution.py:209
  166.6 4.4 all-to-all-start.3
  198.1 3.9 copy.168
  202.0 4.8 %concatenate.66 = f32[64,32,256]{2,1,0:T(8,128)} reshape(f32[64,128,64]{2,1,0:T(8,128)} %copy.168) | data formatting | bytes 4194304 | tf_op jit(solution)/shard_map/concatenate | solution.py:248
  206.9 4.7 %fusion.36 = f32[64,128,64]{1,2,0:T(8,128)} fusion(f32[64,64,128]{2,1,0:T(8,128)} %copy-done.12, f32[64,64,128]{2,1,0:T(8,128)S(1)} %get-tuple-element.50, f32[256,2,128]{2,0,1:T(8,128)S(1)} %bitcast.352), kind=kOutput, calls=%fused_computation.72 | convolution fusion | flops 806354944 | bytes 6422528 | tf_op jit(solution)/shard_map/rcb,bm->rmc/dot_general | solution.py:45
  211.6 3.9 copy.169
  215.5 5.3 %concatenate.67 = f32[64,32,256]{2,1,0:T(8,128)} reshape(f32[64,128,64]{2,1,0:T(8,128)} %copy.169) | data formatting | bytes 4194304 | tf_op jit(solution)/shard_map/concatenate | solution.py:248
  220.8 4.2 maximum_bitcast_fusion.2
  225.1 16.0 %all-to-all-done.3 = f32[32,96,256]{2,1,0:T(8,128)} async-done(((f32[32,96,256]{2,1,0:T(8,128)}), f32[32,96,256]{2,1,0:T(8,128)}, u32[]{:S(2)}, u32[]{:S(2)}) %all-to-all-start.3) | async-done | bytes 3145760 | tf_op jit(solution)/shard_map/all_to_all | solution.py:209
  244.2 4.4 copy.171
  248.7 5.0 %all-to-all-start.4 = ((f32[32,128,256]{2,1,0:T(8,128)}), f32[32,128,256]{2,1,0:T(8,128)}, u32[]{:S(2)}, u32[]{:S(2)}) async-start(f32[32,128,256]{2,1,0:T(8,128)} %copy.171), calls=%async_computation.4 | async-start | bytes 8388608 | tf_op jit(solution)/shard_map/all_to_all | solution.py:250
  276.3 69.5 %all-to-all-done.4 = f32[32,128,256]{2,1,0:T(8,128)} async-done(((f32[32,128,256]{2,1,0:T(8,128)}), f32[32,128,256]{2,1,0:T(8,128)}, u32[]{:S(2)}, u32[]{:S(2)}) %all-to-all-start.4) | async-done | bytes 4194336 | tf_op jit(solution)/shard_map/all_to_all | solution.py:250
  345.8 5.7 %all-to-all-start.5 = ((f32[32,32,256]{2,1,0:T(8,128)}), f32[32,32,256]{2,1,0:T(8,128)S(1)}, u32[]{:S(2)}, u32[]{:S(2)}) async-start(f32[32,32,256]{2,1,0:T(8,128)} %pad_maximum_fusion.31), calls=%async_computation.5 | async-start | bytes 2097152 | tf_op jit(solution)/shard_map/all_to_all | solution.py:209
  360.1 3.5 fusion.49
  364.8 11.6 %all-to-all-done.5 = f32[32,32,256]{2,1,0:T(8,128)S(1)} async-done(((f32[32,32,256]{2,1,0:T(8,128)}), f32[32,32,256]{2,1,0:T(8,128)S(1)}, u32[]{:S(2)}, u32[]{:S(2)}) %all-to-all-start.5) | async-done | bytes 1048608 | tf_op jit(solution)/shard_map/all_to_all | solution.py:209
  381.2 4.9 %all-to-all-start.6 = ((f32[4,128,512]{2,1,0:T(8,128)}), f32[4,128,512]{2,1,0:T(8,128)S(1)}, u32[]{:S(2)}, u32[]{:S(2)}) async-start(f32[4,128,512]{2,1,0:T(8,128)} %bitcast.106), calls=%async_computation.6 | async-start | bytes 2097152 | tf_op jit(solution)/shard_map/all_to_all | solution.py:268
  388.3 24.6 %all-to-all-done.6.transfer_in = f32[4,128,512]{2,1,0:T(8,128)S(1)} async-done(((f32[4,128,512]{2,1,0:T(8,128)}), f32[4,128,512]{2,1,0:T(8,128)S(1)}, u32[]{:S(2)}, u32[]{:S(2)}) %all-to-all-start.6) | async-done | bytes 1048608 | tf_op jit(solution)/shard_map/all_to_all | solution.py:268
  413.8 3.5 all-to-all-start.7
  428.6 10.3 %shard_map.138 = (f32[1024,512]{1,0:T(8,128)}, f32[1024,512]{1,0:T(8,128)}, f32[1024,512]{1,0:T(8,128)}) custom-call(f32[4]{0:T(128)S(1)} %copy-done.9, f32[4]{0:T(128)S(1)} %copy-done.10, f32[4]{0:T(128)S(1)} %copy-done.11, f32[4,128,512]{2,1,0:T(8,128)S(1)} %copy-done.8, f32[1024,512]{1,0:T(8,128)} %slip_rate_in.3, f32[1024,512]{1,0:T(8,128)S(1)} %copy-done, ...), custom_call_target="tpu_custom_call" | custom-call | flops 52428800 | bytes 9437184 | tf_op jit(solution)/shard_map/pallas_call | solution.py:115
  438.9 4.3 all-to-all-done.7.transfer_in
  448.0 10.3 %shard_map.139 = (f32[1024,512]{1,0:T(8,128)}, f32[1024,512]{1,0:T(8,128)}, f32[1024,512]{1,0:T(8,128)}) custom-call(f32[4]{0:T(128)S(1)} %copy-done.9, f32[4]{0:T(128)S(1)} %copy-done.10, f32[4]{0:T(128)S(1)} %copy-done.11, f32[4,128,512]{2,1,0:T(8,128)S(1)} %all-to-all-done.7.transfer_in, ...), custom_call_target="tpu_custom_call", output_to_operand_aliasing={{0}: (9, {}), {1}: (10, {}), {2}: (11, {})} | custom-call | flops 52428800 | bytes 9437184 | tf_op jit(solution)/shard_map/pallas_call | solution.py:115
  (191 shorter events, 120.9 us)
Async XLA Ops:
  0.6 54.6 %all-to-all-start = ((f32[4,256,512]{2,1,0:T(8,128)}), f32[4,256,512]{2,1,0:T(8,128)S(1)}, u32[]{:S(2)}, u32[]{:S(2)}) async-start(f32[4,256,512]{2,1,0:T(8,128)} %bitcast.348), calls=%async_computation | async-start | bytes 4194304 | tf_op jit(solution)/shard_map/all_to_all | solution.py:204
  55.2 52.3 %all-to-all-start.1 = ((f32[4,256,512]{2,1,0:T(8,128)}), f32[4,256,512]{2,1,0:T(8,128)}, u32[]{:S(2)}, u32[]{:S(2)}) async-start(f32[4,256,512]{2,1,0:T(8,128)} %bitcast.35), calls=%async_computation.1 | async-start | bytes 4194304 | tf_op jit(solution)/shard_map/all_to_all | solution.py:204
  60.9 111.1 %copy-start.23 = (f32[128,2,64,1]{0,2,1,3:T(8,128)}, f32[128,2,64,1]{0,2,1,3:T(8,128)S(1)}, u32[]{:S(2)}) copy-start(f32[128,2,64,1]{0,2,1,3:T(8,128)S(1)} %reshape.588) | copy-start | bytes 196612
  63.0 110.5 %copy-start.20 = (f32[2,128,2,128]{3,1,0,2:T(8,128)}, f32[2,128,2,128]{3,1,0,2:T(8,128)S(1)}, u32[]{:S(2)}) copy-start(f32[2,128,2,128]{3,1,0,2:T(8,128)S(1)} %copy.163) | copy-start | bytes 786436
  64.7 108.4 %copy-start.26 = (f32[64,128]{1,0:T(8,128)}, f32[64,128]{1,0:T(8,128)S(1)}, u32[]{:S(2)}) copy-start(f32[64,128]{1,0:T(8,128)S(1)} %get-tuple-element.100) | copy-start | bytes 98308
  107.5 56.7 %all-to-all-start.2 = ((f32[32,66,256]{2,1,0:T(8,128)}), f32[32,66,256]{2,1,0:T(8,128)S(1)}, u32[]{:S(2)}, u32[]{:S(2)}) async-start(f32[32,66,256]{2,1,0:T(8,128)} %pad_maximum_fusion.10), calls=%async_computation.2 | async-start | bytes 4718592 | tf_op jit(solution)/shard_map/all_to_all | solution.py:209
  147.0 7.1 %copy-start.14 = (f32[128,16,256]{2,1,0:T(8,128)}, f32[128,16,256]{2,1,0:T(8,128)S(1)}, u32[]{:S(2)}) copy-start(f32[128,16,256]{2,1,0:T(8,128)S(1)} %copy.158) | copy-start | bytes 6291460
  166.6 74.4 %all-to-all-start.3 = ((f32[32,96,256]{2,1,0:T(8,128)}), f32[32,96,256]{2,1,0:T(8,128)}, u32[]{:S(2)}, u32[]{:S(2)}) async-start(f32[32,96,256]{2,1,0:T(8,128)} %pad_maximum_fusion.6), calls=%async_computation.3 | async-start | bytes 6291456 | tf_op jit(solution)/shard_map/all_to_all | solution.py:209
  183.9 1.8 copy-start.34
  185.7 2.0 copy-start.18
  188.0 1.6 copy-start.17
  190.7 2.0 copy-start.33
  192.7 2.3 copy-start.25
  215.5 5.4 %copy-start.16 = (f32[64,32,256]{2,1,0:T(8,128)S(1)}, f32[64,32,256]{2,1,0:T(8,128)}, u32[]{:S(2)}) copy-start(f32[64,32,256]{2,1,0:T(8,128)} %concatenate.66) | copy-start | bytes 6291460
  241.1 3.1 copy-start.13
  248.7 97.2 %all-to-all-start.4 = ((f32[32,128,256]{2,1,0:T(8,128)}), f32[32,128,256]{2,1,0:T(8,128)}, u32[]{:S(2)}, u32[]{:S(2)}) async-start(f32[32,128,256]{2,1,0:T(8,128)} %copy.171), calls=%async_computation.4 | async-start | bytes 8388608 | tf_op jit(solution)/shard_map/all_to_all | solution.py:250
  271.8 3.2 copy-start.22
  275.0 76.9 %copy-start.29 = (f32[1,128,2,128]{1,3,2,0:T(8,128)S(1)}, f32[1,128,2,128]{1,3,2,0:T(8,128)}, u32[]{:S(2)}) copy-start(f32[1,128,2,128]{1,3,2,0:T(8,128)} %get-tuple-element.72) | copy-start | bytes 393220
  275.0 76.9 %copy-start.30 = (f32[1,128,2,128]{1,3,2,0:T(8,128)S(1)}, f32[1,128,2,128]{1,3,2,0:T(8,128)}, u32[]{:S(2)}) copy-start(f32[1,128,2,128]{1,3,2,0:T(8,128)} %get-tuple-element.75) | copy-start | bytes 393220
  345.8 30.7 %all-to-all-start.5 = ((f32[32,32,256]{2,1,0:T(8,128)}), f32[32,32,256]{2,1,0:T(8,128)S(1)}, u32[]{:S(2)}, u32[]{:S(2)}) async-start(f32[32,32,256]{2,1,0:T(8,128)} %pad_maximum_fusion.31), calls=%async_computation.5 | async-start | bytes 2097152 | tf_op jit(solution)/shard_map/all_to_all | solution.py:209
  356.9 2.0 copy-start.32
  381.2 6.2 %copy-start.19 = (f32[32,4,8,256]{3,2,0,1:T(8,128)S(1)}, f32[32,4,8,256]{3,2,0,1:T(8,128)}, u32[]{:S(2)}) copy-start(f32[32,4,8,256]{3,2,0,1:T(8,128)} %copy.207) | copy-start | bytes 3145732
  381.2 31.6 %all-to-all-start.6 = ((f32[4,128,512]{2,1,0:T(8,128)}), f32[4,128,512]{2,1,0:T(8,128)S(1)}, u32[]{:S(2)}, u32[]{:S(2)}) async-start(f32[4,128,512]{2,1,0:T(8,128)} %bitcast.106), calls=%async_computation.6 | async-start | bytes 2097152 | tf_op jit(solution)/shard_map/all_to_all | solution.py:268
  388.3 29.1 %copy-start.28 = (f32[64,128]{1,0:T(8,128)S(1)}, f32[64,128]{1,0:T(8,128)}, u32[]{:S(2)}) copy-start(f32[64,128]{1,0:T(8,128)} %copy-done.26) | copy-start | bytes 98308
  413.8 29.4 %all-to-all-start.7 = ((f32[4,128,512]{2,1,0:T(8,128)}), f32[4,128,512]{2,1,0:T(8,128)S(1)}, u32[]{:S(2)}, u32[]{:S(2)}) async-start(f32[4,128,512]{2,1,0:T(8,128)} %bitcast.104), calls=%async_computation.7 | async-start | bytes 2097152 | tf_op jit(solution)/shard_map/all_to_all | solution.py:268
  417.5 6.7 %copy-start.9 = (f32[4]{0:T(128)S(1)}, f32[4]{0:T(128)}, u32[]{:S(2)}) copy-start(f32[4]{0:T(128)} %rate_coef.3) | copy-start | bytes 52
  417.5 6.6 %copy-start.10 = (f32[4]{0:T(128)S(1)}, f32[4]{0:T(128)}, u32[]{:S(2)}) copy-start(f32[4]{0:T(128)} %state_coef.3) | copy-start | bytes 52
  417.5 6.6 %copy-start.11 = (f32[4]{0:T(128)S(1)}, f32[4]{0:T(128)}, u32[]{:S(2)}) copy-start(f32[4]{0:T(128)} %slip_scale.3) | copy-start | bytes 52
  421.0 3.2 copy-start
  421.0 3.2 copy-start.1
  424.2 1.6 copy-start.3
  443.2 1.6 copy-start.2
  (11 other events, 13.8 us)
